TPU v7x, 512 devices: a whole 4x8x8 slice. The times are simulated.
512 devices in a mesh: expert: 128 (over y, z, core), dp: 4 (over x).
Axes of the slice: x: 4, y: 8, z: 8, core: 2. Of those that a mesh axis runs over, the one named last changes fastest.
Arguments:
- hidden: bfloat16 [128, 4, 256, 1024], P('expert', 'dp'), may hold values from -6 to 6
- w_down: bfloat16 [128, 1024, 3584], P('expert', 'dp'), may hold values from -0.1875 to 0.1875
- expert_ids: int32 [4, 2048, 8], P('dp', 'expert'), may hold values from 0 to 127, all different within a row; in each aligned block of 16 rows (0 to 15, 16 to 31, ..., all dimensions but the last counted through in order) at most 2 rows name the same one
- route_weights: float32 [4, 2048, 8], P('dp', 'expert'), may hold values from 0.1 to 0.6
- grad_out: bfloat16 [4, 2048, 3584], P('dp', 'expert'), may hold values from -6 to 6
Outputs:
- mixed: bfloat16 [4, 2048, 3584], P('dp', 'expert')
- d_hidden: bfloat16 [128, 4, 256, 1024], P('expert', 'dp')
- d_w_down: bfloat16 [128, 1024, 3584], P('expert', 'dp')
- d_route: float32 [4, 2048, 8], P('dp', 'expert')
Inputs may be any that keep to these rules, and one draw needn't show every extreme that they name: `expert_ids`: among the 16 tokens of one device no expert is chosen more than 2 times, and some expert is chosen exactly 2 times; the 8 choices of a token are distinct.
All inputs are finite; a program needn't handle non-finite values.
Results may differ from a plain program's by a relative error of at most 0.0085.
Values may be sent and summed in bfloat16 or wider, within the bound.
A program may use at most 128 MiB of HBM per device.

v0:
```python
import jax
import jax.numpy as jnp
from jax import lax
from jax.sharding import PartitionSpec as P


def slot_ranks(choices, experts):
    flat = choices.reshape(-1)
    onehot = (flat[:, None] == jnp.arange(experts, dtype=jnp.int32)[None, :]).astype(jnp.int32)
    earlier = jnp.cumsum(onehot, axis=0) - onehot
    return jnp.sum(earlier * onehot, axis=1).reshape(choices.shape)


def on_device(hidden, w_down, expert_ids, route_weights, grad_out):
    experts = lax.axis_size("expert")
    groups = lax.axis_size("dp")
    slots = hidden.shape[2] // experts
    width = w_down.shape[2]
    w_whole = lax.all_gather(w_down, "dp", axis=1, tiled=True)[0]
    out_slots = jnp.dot(hidden[0, 0], w_whole, preferred_element_type=jnp.float32).astype(
        jnp.bfloat16
    )
    arrived = lax.all_to_all(
        out_slots.reshape(experts, slots, width), "expert", split_axis=0, concat_axis=0, tiled=True
    )
    arrived = arrived.reshape(experts * slots, width)
    choices = expert_ids[0]
    weights = route_weights[0]
    cotangent = grad_out[0].astype(jnp.float32)
    rows = choices * slots + slot_ranks(choices, experts)
    out_pair = arrived[rows].astype(jnp.float32)
    mixed = jnp.einsum("tk,tkd->td", weights, out_pair)
    d_route = jnp.einsum("td,tkd->tk", cotangent, out_pair)
    grad_pair = (weights[..., None] * cotangent[:, None, :]).astype(jnp.bfloat16)
    outgoing = jnp.zeros((experts * slots, width), jnp.bfloat16)
    outgoing = outgoing.at[rows.reshape(-1)].set(grad_pair.reshape(-1, width))
    mine = lax.all_to_all(
        outgoing.reshape(experts, 1, slots, width),
        "expert",
        split_axis=0,
        concat_axis=0,
        tiled=True,
    )
    own_grads = mine[:, 0]
    slot_grads = lax.all_gather(mine, "dp", axis=1, tiled=True)
    d_hidden = jnp.einsum(
        "rd,hd->rh", own_grads.reshape(-1, width), w_whole, preferred_element_type=jnp.float32
    ).astype(jnp.bfloat16)
    columns = lax.all_to_all(hidden, "dp", split_axis=3, concat_axis=1, tiled=True)[0]
    columns = columns.reshape(groups, experts, slots, columns.shape[-1])
    d_weight = jnp.einsum(
        "gsch,sgcd->hd", columns, slot_grads, preferred_element_type=jnp.float32
    ).astype(jnp.bfloat16)
    return (
        mixed.astype(jnp.bfloat16)[None],
        d_hidden.reshape(hidden.shape),
        d_weight[None],
        d_route[None],
    )


def solution(mesh):
    placed = (
        P("expert", "dp", None, None),
        P("expert", "dp", None),
        P("dp", "expert", None),
        P("dp", "expert", None),
        P("dp", "expert", None),
    )
    return jax.shard_map(
        on_device,
        mesh=mesh,
        in_specs=placed,
        out_specs=(
            P("dp", "expert", None),
            P("expert", "dp", None, None),
            P("expert", "dp", None),
            P("dp", "expert", None),
        ),
        check_vma=False,
    )
```

profile of v0, /device:TPU:1, one launch (start us, length us, event | category | flops | bytes accessed | tf_op | source)
XLA Modules:
  0.0 197.7 jit_solution(9017277390061045914)
XLA Ops:
  7.2 0.0 all-gather.3.cloned.1.call-start
  7.2 0.7 all-gather.3.cloned.1.call-update
  7.9 0.0 all-gather.5.cloned.1.call-start
  8.0 0.1 copy.46
  8.1 0.1 eq.15
  8.2 0.1 copy.49
  8.2 0.1 mul.52
  8.3 0.1 copy.50
  8.4 0.1 mul.53
  8.5 0.1 fusion.29
  8.6 0.2 reduce_window_sum.11
  8.8 0.2 select_reduce_fusion
  9.0 2.5 %scatter_custom_fusion = bf16[256,3584]{1,0:T(8,128)(2,1)S(1)} fusion(s32[128]{0:T(128)S(1)} %fusion.30, f32[16,3584]{1,0:T(8,128)S(1)} %bitcast_convert_fusion.1, f32[128]{0:T(128)S(1)} %mul.53, bf16[]{:T(256)} %constant.7.clone.1), kind=kCustom, calls=%fused_computation.14 | custom fusion | flops 917504 | bytes 2064898 | tf_op jit(solution)/shard_map/scatter | solution.py:36
  11.5 1.6 reshape.99
  13.2 64.9 %all_to_all.25 = bf16[128,1,2,3584]{3,2,1,0:T(2,128)(2,1)S(1)} all-to-all(bf16[128,1,2,3584]{3,2,1,0:T(2,128)(2,1)} %bitcast.75), channel_id=1, replica_groups=mesh['expert'=128,'dp'=4] {'expert'}, dimensions={0} | all-to-all | bytes 3670016 | tf_op jit(solution)/shard_map/all_to_all | solution.py:37
  78.1 3.7 %copy.52 = bf16[128,1,2,3584]{0,3,1,2:T(8,128)(2,1)} copy(bf16[128,1,2,3584]{3,2,1,0:T(2,128)(2,1)S(1)} %all_to_all.25) | data formatting | bytes 3670016 | tf_op jit(solution)/shard_map/all_to_all | solution.py:37
  81.8 0.0 all-gather.5.cloned.1.call-update
  81.8 1.0 copy-done
  82.8 0.8 copy.53
  83.7 0.5 broadcast.58
  84.2 3.8 %reduce = bf16[1024,256]{1,0:T(8,128)(2,1)S(1)} reduce(bf16[1024,1,1,256]{3,2,1,0:T(2,128)(2,1)S(1)} %bitcast.77, bf16[]{:T(256)} %broadcast.58), dimensions={1,2}, to_apply=%bitcast.68.reduce_sub_computation | reduce | bytes 1048578
  88.0 0.0 copy-start.1
  88.0 0.9 reshape.125
  88.9 4.0 %all-to-all-start.2 = ((bf16[4,2,32768]{2,1,0:T(2,128)(2,1)}), bf16[4,2,32768]{2,1,0:T(2,128)(2,1)S(1)}, u32[]{:S(2)}, u32[]{:S(2)}) async-start(bf16[4,2,32768]{2,1,0:T(2,128)(2,1)} %reshape.125), calls=%async_computation.2 | async-start | bytes 1048576 | tf_op jit(solution)/shard_map/all_to_all | solution.py:49
  93.0 2.2 %all-gather.3.cloned.1.call-done = bf16[1,1024,3584]{2,1,0:T(8,128)(2,1)} async-done(((bf16[1,256,3584]{2,1,0:T(8,128)(2,1)}), bf16[1,1024,3584]{2,1,0:T(8,128)(2,1)}) %all-gather.3.cloned.1.call-update) | async-done | bytes 7340048 | tf_op jit(solution)/shard_map/all_gather | solution.py:19
  95.1 6.4 %fusion.5 = bf16[256,3584]{1,0:T(8,128)(2,1)} fusion(bf16[1,1024,3584]{2,1,0:T(8,128)(2,1)} %all-gather.3.cloned.1.call-done, bf16[1,1,256,1024]{3,2,1,0:T(8,128)(2,1)S(1)} %copy-done.1), kind=kOutput, calls=%fused_computation.8 | convolution fusion | flops 1879965696 | bytes 9699328 | tf_op jit(solution)/shard_map/dot_general | solution.py:20
  101.5 4.7 %reshape.96 = bf16[128,2,3584]{2,1,0:T(2,128)(2,1)} reshape(bf16[256,3584]{1,0:T(8,128)(2,1)} %fusion.5) | data formatting | bytes 3670016 | tf_op jit(solution)/shard_map/reshape | solution.py:24
  106.2 20.2 %all-to-all-start = ((bf16[128,2,3584]{2,1,0:T(2,128)(2,1)}), bf16[128,2,3584]{2,1,0:T(2,128)(2,1)}, u32[]{:S(2)}, u32[]{:S(2)}) async-start(bf16[128,2,3584]{2,1,0:T(2,128)(2,1)} %reshape.96), calls=%async_computation | async-start | bytes 3670016 | tf_op jit(solution)/shard_map/all_to_all | solution.py:23
  126.5 0.1 reshape.98
  126.5 0.1 copy.47
  126.6 0.1 copy.48
  126.7 0.1 reshape.103
  126.8 0.1 copy.57
  126.9 0.5 reshape.126
  127.4 0.1 copy.62
  127.5 0.3 copy.54
  127.8 1.6 reshape_squeeze.6
  129.5 6.6 %fusion.13 = bf16[1,1,256,1024]{3,2,1,0:T(8,128)(2,1)} fusion(bf16[256,3584]{1,0:T(8,128)(2,1)} %reshape_squeeze.6, bf16[1,1024,3584]{2,1,0:T(8,128)(2,1)} %all-gather.3.cloned.1.call-done), kind=kOutput, calls=%fused_computation.13 | convolution fusion | flops 1879310336 | bytes 9699328 | tf_op jit(solution)/shard_map/rd,hd->rh/dot_general | solution.py:46
  136.1 36.5 %all-to-all-done = bf16[128,2,3584]{2,1,0:T(2,128)(2,1)} async-done(((bf16[128,2,3584]{2,1,0:T(2,128)(2,1)}), bf16[128,2,3584]{2,1,0:T(2,128)(2,1)}, u32[]{:S(2)}, u32[]{:S(2)}) %all-to-all-start) | async-done | bytes 1835040 | tf_op jit(solution)/shard_map/all_to_all | solution.py:23
  172.6 4.1 %reshape.97 = bf16[256,3584]{1,0:T(8,128)(2,1)S(1)} reshape(bf16[128,2,3584]{2,1,0:T(2,128)(2,1)} %all-to-all-done) | data formatting | bytes 3670016 | tf_op jit(solution)/shard_map/reshape | solution.py:26
  176.7 1.1 gather_fusion
  177.8 0.4 fusion.18
  178.2 0.7 copy.70
  178.9 0.6 fusion.20
  179.5 0.7 copy.61
  180.2 3.0 %all-gather.5.cloned.1.call-done = bf16[128,4,2,3584]{0,3,1,2:T(8,128)(2,1)} async-done(((bf16[128,1,2,3584]{0,3,1,2:T(8,128)(2,1)}), bf16[128,4,2,3584]{0,3,1,2:T(8,128)(2,1)}) %all-gather.5.cloned.1.call-update) | async-done | bytes 7340048 | tf_op jit(solution)/shard_map/all_gather | solution.py:45
  183.1 5.2 %fusion.8 = bf16[1,256,3584]{1,2,0:T(8,128)(2,1)S(1)} fusion(bf16[128,4,2,3584]{0,3,1,2:T(8,128)(2,1)} %all-gather.5.cloned.1.call-done, bf16[4,128,2,256]{3,0,2,1:T(4,128)(2,1)S(1)} %bitcast.79), kind=kOutput, calls=%fused_computation.9 | convolution fusion | flops 1879965696 | bytes 9699328 | tf_op jit(solution)/shard_map/gsch,sgcd->hd/dot_general | solution.py:51
  188.3 2.6 %copy.56 = bf16[1,256,3584]{2,1,0:T(8,128)(2,1)} copy(bf16[1,256,3584]{1,2,0:T(8,128)(2,1)S(1)} %fusion.8) | data formatting | bytes 3670016
  (14 shorter events, 0.1 us)
Async XLA Ops:
  7.2 0.8 copy-start.3
  7.2 1.1 copy-start.4
  7.2 1.8 copy-start.2
  7.2 87.9 %all-gather.3.cloned.1.call-start = ((), (), s32[]{:S(2)}) async-start(), calls=%async_computation.3 | async-start | bytes 9175040 | tf_op jit(solution)/shard_map/all_gather | solution.py:19
  7.9 175.2 %all-gather.5.cloned.1.call-start = ((), (), s32[]{:S(2)}) async-start(), calls=%async_computation.4 | async-start | bytes 9175040 | tf_op jit(solution)/shard_map/all_gather | solution.py:45
  81.8 1.0 copy-start
  88.0 7.1 %copy-start.1 = (bf16[1,1,256,1024]{3,2,1,0:T(8,128)(2,1)S(1)}, bf16[1,1,256,1024]{3,2,1,0:T(8,128)(2,1)}, u32[]{:S(2)}) copy-start(bf16[1,1,256,1024]{3,2,1,0:T(8,128)(2,1)} %param.5) | copy-start | bytes 1572868
  88.9 17.3 %all-to-all-start.2 = ((bf16[4,2,32768]{2,1,0:T(2,128)(2,1)}), bf16[4,2,32768]{2,1,0:T(2,128)(2,1)S(1)}, u32[]{:S(2)}, u32[]{:S(2)}) async-start(bf16[4,2,32768]{2,1,0:T(2,128)(2,1)} %reshape.125), calls=%async_computation.2 | async-start | bytes 1048576 | tf_op jit(solution)/shard_map/all_to_all | solution.py:49
  106.2 66.4 %all-to-all-start = ((bf16[128,2,3584]{2,1,0:T(2,128)(2,1)}), bf16[128,2,3584]{2,1,0:T(2,128)(2,1)}, u32[]{:S(2)}, u32[]{:S(2)}) async-start(bf16[128,2,3584]{2,1,0:T(2,128)(2,1)} %reshape.96), calls=%async_computation | async-start | bytes 3670016 | tf_op jit(solution)/shard_map/all_to_all | solution.py:23
Sparse Core Ops, SparseCore 0:
  10.1 84.9 all-gather.2
  97.2 85.8 all-gather.4
where the time goes:
time: 198 us
  blocking collectives  64.9 us (33%)
  waiting for transfers between devices  42.3 us (21%)
  local copies, waits for them, and re-layouts  25.9 us (13%)
  starting transfers between devices  24.3 us (12%)
  matrix products  19.2 us (10%)
  between operations  14.2 us (7%)
  other arithmetic  6.83 us (3%)
    all_to_all x1, blocking collectives, on_device(): lax.all_to_all(outgoing.reshape(experts, 1, slots, width), 'expert', spli...  64.9 us
    all_to_all x1, waiting for transfers between devices, on_device(): lax.all_to_all(out_slots.reshape(experts, slots, width), 'expert', split_...  36.5 us
    all_to_all x1, starting transfers between devices, on_device(): lax.all_to_all(out_slots.reshape(experts, slots, width), 'expert', split_...  20.2 us
    dot_general x1, matrix products, on_device(): jnp.einsum('rd,hd->rh', own_grads.reshape(-1, width), w_whole, preferred_...  6.64 us
    unnamed x18, local copies, waits for them, and re-layouts  6.64 us
    dot_general x1, matrix products, on_device(): jnp.dot(hidden[0, 0], w_whole, preferred_element_type=jnp.float32)  6.37 us
    dot_general x1, matrix products, on_device(): jnp.einsum('gsch,sgcd->hd', columns, slot_grads, preferred_element_type=j...  5.17 us
    reshape x1, local copies, waits for them, and re-layouts, on_device(): out_slots.reshape(experts, slots, width)  4.75 us
  transfers between devices with their start and end apart: 4, of which 3 were waited for; matrix products, arithmetic and copies ran while one was open for 22% of the time, Pallas kernels for 0%

commit v1 on v0

--- a/solution.py
+++ b/solution.py
@@ -46,7 +46,15 @@
     d_hidden = jnp.einsum(
         "rd,hd->rh", own_grads.reshape(-1, width), w_whole, preferred_element_type=jnp.float32
     ).astype(jnp.bfloat16)
-    columns = lax.all_to_all(hidden, "dp", split_axis=3, concat_axis=1, tiled=True)[0]
+    columns = jnp.concatenate(
+        lax.all_to_all(
+            jnp.stack(jnp.split(hidden, lax.psum(1, axis_name="dp"), 3), axis=0),
+            split_axis=0,
+            axis_name="dp",
+            concat_axis=0,
+        ),
+        1,
+    )[0]
     columns = columns.reshape(groups, experts, slots, columns.shape[-1])
     d_weight = jnp.einsum(
         "gsch,sgcd->hd", columns, slot_grads, preferred_element_type=jnp.float32

time: 198 us -> 197 us (level)
  waiting for transfers between devices: 42.3 us -> 55.5 us
  local copies, waits for them, and re-layouts: 25.9 us -> 18.3 us
  starting transfers between devices: 24.3 us -> 19.5 us
  other arithmetic: 6.83 us -> 3.87 us
    all_gather x1, waiting for transfers between devices: 2.16 us -> 14.8 us  [on_device(): w_whole = lax.all_gather(w_down, 'dp', axis=1, tiled=True)[0]]
    unnamed x18 -> x10, local copies, waits for them, and re-layouts: 6.64 us -> 1.17 us
    all_to_all x1, starting transfers between devices: 20.2 us -> 15.4 us  [on_device(): lax.all_to_all(out_slots.reshape(experts, slots, width), 'expert', split_...]
    unnamed x1 -> x0, other arithmetic: 3.82 us -> none
    all_to_all x1, local copies, waits for them, and re-layouts: 3.72 us -> 1.42 us  [on_device(): lax.all_to_all(outgoing.reshape(experts, 1, slots, width), 'expert', spli...]
  transfers between devices with their start and end apart: 4 -> 4, of which waited for: 3 -> 3; matrix products, arithmetic and copies ran while one was open for 22% -> 18% of each run, Pallas kernels for 0% -> 0%
where the time goes in v1:
time: 197 us
  blocking collectives  64.9 us (33%)
  waiting for transfers between devices  55.5 us (28%)
  matrix products  20.4 us (10%)
  starting transfers between devices  19.5 us (10%)
  local copies, waits for them, and re-layouts  18.3 us (9%)
  between operations  14.2 us (7%)
  other arithmetic  3.87 us (2%)
    all_to_all x1, blocking collectives, on_device(): lax.all_to_all(outgoing.reshape(experts, 1, slots, width), 'expert', spli...  64.9 us
    all_to_all x1, waiting for transfers between devices, on_device(): lax.all_to_all(out_slots.reshape(experts, slots, width), 'expert', split_...  37 us
    all_to_all x1, starting transfers between devices, on_device(): lax.all_to_all(out_slots.reshape(experts, slots, width), 'expert', split_...  15.4 us
    all_gather x1, waiting for transfers between devices, on_device(): w_whole = lax.all_gather(w_down, 'dp', axis=1, tiled=True)[0]  14.8 us
    dot_general x1, matrix products, on_device(): jnp.einsum('rd,hd->rh', own_grads.reshape(-1, width), w_whole, preferred_...  6.67 us
    dot_general x1, matrix products, on_device(): jnp.einsum('gsch,sgcd->hd', columns, slot_grads, preferred_element_type=j...  6.41 us
    dot_general x1, matrix products, on_device(): jnp.dot(hidden[0, 0], w_whole, preferred_element_type=jnp.float32)  6.37 us
    reshape x1, local copies, waits for them, and re-layouts, on_device(): out_slots.reshape(experts, slots, width)  4.75 us
  transfers between devices with their start and end apart: 4, of which 3 were waited for; matrix products, arithmetic and copies ran while one was open for 18% of the time, Pallas kernels for 0%

profile of v1, /device:TPU:1, one launch (start us, length us, event | category | flops | bytes accessed | tf_op | source)
XLA Modules:
  0.0 196.7 jit_solution(11578618305341478751)
XLA Ops:
  7.2 0.0 copy-start.2
  7.2 0.0 copy-start.3
  7.2 0.0 copy-start.1
  7.2 0.0 all-gather.3.cloned.1.call-start
  7.2 0.7 all-gather.3.cloned.1.call-update
  7.9 0.0 all-gather.5.cloned.1.call-start
  8.0 0.0 copy-done.2
  8.0 0.1 copy.32
  8.1 0.1 eq.15
  8.2 0.1 copy.35
  8.2 0.1 mul.52
  8.3 0.0 copy-done.3
  8.3 0.1 copy.36
  8.4 0.1 mul.53
  8.5 0.1 fusion.29
  8.6 0.2 reduce_window_sum.11
  8.8 0.2 select_reduce_fusion
  8.9 0.0 copy-done.1
  9.0 2.5 %scatter_custom_fusion = bf16[256,3584]{1,0:T(8,128)(2,1)S(1)} fusion(s32[128]{0:T(128)S(1)} %fusion.30, f32[16,3584]{1,0:T(8,128)S(1)} %bitcast_convert_fusion.1, f32[128]{0:T(128)S(1)} %mul.53, bf16[]{:T(256)} %constant.7.clone.1), kind=kCustom, calls=%fused_computation.14 | custom fusion | flops 917504 | bytes 2064898 | tf_op jit(solution)/shard_map/scatter | solution.py:36
  11.5 1.6 reshape.98
  13.2 64.9 %all_to_all.15 = bf16[128,1,2,3584]{3,2,1,0:T(2,128)(2,1)S(1)} all-to-all(bf16[128,1,2,3584]{3,2,1,0:T(2,128)(2,1)} %bitcast.76), channel_id=1, replica_groups=mesh['expert'=128,'dp'=4] {'expert'}, dimensions={0} | all-to-all | bytes 3670016 | tf_op jit(solution)/shard_map/all_to_all | solution.py:37
  78.1 1.4 copy.39
  79.5 0.0 all-gather.5.cloned.1.call-update
  79.5 1.0 copy-done
  80.6 0.9 pad_maximum_fusion
  81.4 4.0 %all-to-all-start.2 = ((bf16[4,1,1,256,256]{4,3,2,1,0:T(8,128)(2,1)}), bf16[4,1,1,256,256]{4,3,2,1,0:T(8,128)(2,1)S(1)}, u32[]{:S(2)}, u32[]{:S(2)}) async-start(bf16[4,1,1,256,256]{4,3,2,1,0:T(8,128)(2,1)} %pad_maximum_fusion), calls=%async_computation.2 | async-start | bytes 1048576 | tf_op jit(solution)/shard_map/all_to_all | solution.py:50
  85.4 14.8 %all-gather.3.cloned.1.call-done = bf16[1,1024,3584]{2,1,0:T(8,128)(2,1)} async-done(((bf16[1,256,3584]{2,1,0:T(8,128)(2,1)}), bf16[1,1024,3584]{2,1,0:T(8,128)(2,1)}) %all-gather.3.cloned.1.call-update) | async-done | bytes 7340048 | tf_op jit(solution)/shard_map/all_gather | solution.py:19
  100.2 6.4 %fusion.5 = bf16[256,3584]{1,0:T(8,128)(2,1)} fusion(bf16[1,1024,3584]{2,1,0:T(8,128)(2,1)} %all-gather.3.cloned.1.call-done, bf16[1,1,256,1024]{3,2,1,0:T(8,128)(2,1)S(1)} %copy-done), kind=kOutput, calls=%fused_computation.8 | convolution fusion | flops 1879965696 | bytes 9699328 | tf_op jit(solution)/shard_map/dot_general | solution.py:20
  106.6 4.8 %reshape.95 = bf16[128,2,3584]{2,1,0:T(2,128)(2,1)} reshape(bf16[256,3584]{1,0:T(8,128)(2,1)} %fusion.5) | data formatting | bytes 3670016 | tf_op jit(solution)/shard_map/reshape | solution.py:24
  111.3 0.0 all-to-all-done.2
  111.3 15.4 %all-to-all-start = ((bf16[128,2,3584]{2,1,0:T(2,128)(2,1)}), bf16[128,2,3584]{2,1,0:T(2,128)(2,1)}, u32[]{:S(2)}, u32[]{:S(2)}) async-start(bf16[128,2,3584]{2,1,0:T(2,128)(2,1)} %reshape.95), calls=%async_computation | async-start | bytes 3670016 | tf_op jit(solution)/shard_map/all_to_all | solution.py:23
  126.7 0.1 reshape.97
  126.8 0.1 copy.41
  126.9 0.1 copy.33
  127.0 0.1 copy.34
  127.1 0.1 reshape.102
  127.2 0.4 copy.38
  127.6 1.6 reshape_squeeze.3
  129.2 6.7 %fusion.13 = bf16[1,1,256,1024]{3,2,1,0:T(8,128)(2,1)} fusion(bf16[256,3584]{1,0:T(8,128)(2,1)} %reshape_squeeze.3, bf16[1,1024,3584]{2,1,0:T(8,128)(2,1)} %all-gather.3.cloned.1.call-done), kind=kOutput, calls=%fused_computation.13 | convolution fusion | flops 1879310336 | bytes 9699328 | tf_op jit(solution)/shard_map/rd,hd->rh/dot_general | solution.py:46
  135.9 37.0 %all-to-all-done = bf16[128,2,3584]{2,1,0:T(2,128)(2,1)} async-done(((bf16[128,2,3584]{2,1,0:T(2,128)(2,1)}), bf16[128,2,3584]{2,1,0:T(2,128)(2,1)}, u32[]{:S(2)}, u32[]{:S(2)}) %all-to-all-start) | async-done | bytes 1835040 | tf_op jit(solution)/shard_map/all_to_all | solution.py:23
  172.9 4.1 %reshape.96 = bf16[256,3584]{1,0:T(8,128)(2,1)S(1)} reshape(bf16[128,2,3584]{2,1,0:T(2,128)(2,1)} %all-to-all-done) | data formatting | bytes 3670016 | tf_op jit(solution)/shard_map/reshape | solution.py:26
  177.0 1.1 gather_fusion
  178.1 0.4 fusion.18
  178.5 0.7 copy.53
  179.2 0.6 fusion.20
  179.7 0.7 copy.45
  180.4 3.0 %all-gather.5.cloned.1.call-done = bf16[128,4,2,3584]{3,0,1,2:T(8,128)(2,1)} async-done(((bf16[128,1,2,3584]{3,0,1,2:T(8,128)(2,1)}), bf16[128,4,2,3584]{3,0,1,2:T(8,128)(2,1)}) %all-gather.5.cloned.1.call-update) | async-done | bytes 7340048 | tf_op jit(solution)/shard_map/all_gather | solution.py:45
  183.4 6.4 %fusion.8 = bf16[1,256,3584]{2,1,0:T(8,128)(2,1)} fusion(bf16[128,4,2,3584]{3,0,1,2:T(8,128)(2,1)} %all-gather.5.cloned.1.call-done, bf16[4,128,2,256]{3,0,2,1:T(4,128)(2,1)S(1)} %bitcast.77), kind=kOutput, calls=%fused_computation.9 | convolution fusion | flops 1879965696 | bytes 9699328 | tf_op jit(solution)/shard_map/gsch,sgcd->hd/dot_general | solution.py:59
  (7 shorter events, 0.1 us)
Async XLA Ops:
  7.2 0.8 copy-start.2
  7.2 1.1 copy-start.3
  7.2 1.8 copy-start.1
  7.2 93.0 %all-gather.3.cloned.1.call-start = ((), (), s32[]{:S(2)}) async-start(), calls=%async_computation.3 | async-start | bytes 9175040 | tf_op jit(solution)/shard_map/all_gather | solution.py:19
  7.9 175.5 %all-gather.5.cloned.1.call-start = ((), (), s32[]{:S(2)}) async-start(), calls=%async_computation.4 | async-start | bytes 9175040 | tf_op jit(solution)/shard_map/all_gather | solution.py:45
  79.5 1.0 copy-start
  81.4 29.9 %all-to-all-start.2 = ((bf16[4,1,1,256,256]{4,3,2,1,0:T(8,128)(2,1)}), bf16[4,1,1,256,256]{4,3,2,1,0:T(8,128)(2,1)S(1)}, u32[]{:S(2)}, u32[]{:S(2)}) async-start(bf16[4,1,1,256,256]{4,3,2,1,0:T(8,128)(2,1)} %pad_maximum_fusion), calls=%async_computation.2 | async-start | bytes 1048576 | tf_op jit(solution)/shard_map/all_to_all | solution.py:50
  111.3 61.6 %all-to-all-start = ((bf16[128,2,3584]{2,1,0:T(2,128)(2,1)}), bf16[128,2,3584]{2,1,0:T(2,128)(2,1)}, u32[]{:S(2)}, u32[]{:S(2)}) async-start(bf16[128,2,3584]{2,1,0:T(2,128)(2,1)} %reshape.95), calls=%async_computation | async-start | bytes 3670016 | tf_op jit(solution)/shard_map/all_to_all | solution.py:23
Sparse Core Ops, SparseCore 0:
  10.1 90.0 all-gather.2
  102.3 81.0 all-gather.4
